TPU v7x, 32 devices: a whole 2x2x4 slice. The times are simulated.
32 devices in a mesh: dp: 8 (over z, x), mp: 4 (over y, core).
Axes of the slice: x: 2, y: 2, z: 4, core: 2. Of those that a mesh axis runs over, the one named last changes fastest.
Arguments:
- interface: float32 [8192, 512], P(('dp', 'mp')), may hold values from -6 to 6
- latents: float32 [1024, 1024], P(('dp', 'mp')), may hold values from -6 to 6
- keep_mask: int32 [8, 1024], P('dp'), may hold values from 0 to 1, as said below
- read_gain_lat: float32 [1024], replicated, may hold values from 0.25 to 1.75
- read_gain_int: float32 [512], replicated, may hold values from 0.25 to 1.75
- read_query: float32 [1024, 1024], P(None, 'mp'), may hold values from -0.1875 to 0.1875
- read_keyval: float32 [2, 512, 1024], P(None, None, 'mp'), may hold values from -0.25 to 0.25
- read_out: float32 [1024, 1024], P('mp'), may hold values from -3 to 3
- read_gain_mlp: float32 [1024], replicated, may hold values from 0.25 to 1.75
- read_up: float32 [1024, 4096], P(None, 'mp'), may hold values from -0.1875 to 0.1875
- read_down: float32 [4096, 1024], P('mp'), may hold values from -0.09375 to 0.09375
- self_gain_att: float32 [2, 1024], replicated, may hold values from 0.25 to 1.75
- self_qkv: float32 [2, 3, 1024, 1024], P(None, None, None, 'mp'), may hold values from -0.1875 to 0.1875
- self_out: float32 [2, 1024, 1024], P(None, 'mp'), may hold values from -1.5 to 1.5
- self_gain_mlp: float32 [2, 1024], replicated, may hold values from 0.25 to 1.75
- self_up: float32 [2, 1024, 4096], P(None, None, 'mp'), may hold values from -0.1875 to 0.1875
- self_down: float32 [2, 4096, 1024], P(None, 'mp'), may hold values from -0.09375 to 0.09375
- write_gain_int: float32 [512], replicated, may hold values from 0.25 to 1.75
- write_gain_lat: float32 [1024], replicated, may hold values from 0.25 to 1.75
- write_query: float32 [512, 512], P(None, 'mp'), may hold values from -0.25 to 0.25
- write_keyval: float32 [2, 1024, 512], P(None, None, 'mp'), may hold values from -0.1875 to 0.1875
- write_out: float32 [512, 512], P('mp'), may hold values from -1.5 to 1.5
- write_gain_mlp: float32 [512], replicated, may hold values from 0.25 to 1.75
- write_up: float32 [512, 2048], P(None, 'mp'), may hold values from -0.25 to 0.25
- write_down: float32 [2048, 512], P('mp'), may hold values from -0.125 to 0.125
- grad_interface_out: float32 [8192, 512], P(('dp', 'mp')), may hold values from -6 to 6
- grad_latents_out: float32 [1024, 1024], P(('dp', 'mp')), may hold values from -6 to 6
Outputs:
- interface_out: float32 [8192, 512], P(('dp', 'mp'))
- latents_out: float32 [1024, 1024], P(('dp', 'mp'))
- grad_interface: float32 [8192, 512], P(('dp', 'mp'))
- grad_latents: float32 [1024, 1024], P(('dp', 'mp'))
- grad_read_gain_lat: float32 [1024], replicated
- grad_read_gain_int: float32 [512], replicated
- grad_read_query: float32 [1024, 1024], P(None, 'mp')
- grad_read_keyval: float32 [2, 512, 1024], P(None, None, 'mp')
- grad_read_out: float32 [1024, 1024], P('mp')
- grad_read_gain_mlp: float32 [1024], replicated
- grad_read_up: float32 [1024, 4096], P(None, 'mp')
- grad_read_down: float32 [4096, 1024], P('mp')
- grad_self_gain_att: float32 [2, 1024], replicated
- grad_self_qkv: float32 [2, 3, 1024, 1024], P(None, None, None, 'mp')
- grad_self_out: float32 [2, 1024, 1024], P(None, 'mp')
- grad_self_gain_mlp: float32 [2, 1024], replicated
- grad_self_up: float32 [2, 1024, 4096], P(None, None, 'mp')
- grad_self_down: float32 [2, 4096, 1024], P(None, 'mp')
- grad_write_gain_int: float32 [512], replicated
- grad_write_gain_lat: float32 [1024], replicated
- grad_write_query: float32 [512, 512], P(None, 'mp')
- grad_write_keyval: float32 [2, 1024, 512], P(None, None, 'mp')
- grad_write_out: float32 [512, 512], P('mp')
- grad_write_gain_mlp: float32 [512], replicated
- grad_write_up: float32 [512, 2048], P(None, 'mp')
- grad_write_down: float32 [2048, 512], P('mp')
Inputs may be any that keep to these rules, and one draw needn't show every extreme that they name: `keep_mask`: each image keeps one patch or more.
All inputs are finite; a program needn't handle non-finite values.
Results may differ from a plain program's by a relative error of at most 0.0003.
Values sent between devices are 32-bit elements; how exact they have to be, the bound alone decides.
No kernel may reach another device: no remote copies, remote signals or barrier semaphores. Data moves between devices by JAX's collectives and lax.ppermute only.
A program may use at most 256 MiB of HBM per device.

v0:
```python
import math
import jax
import jax.numpy as jnp
from jax import lax
from jax.sharding import PartitionSpec as P

D = 1024
E = 512
HEADS = 16
LATENTS = 128
LAYERS = 2
EPSILON = 1e-05
PRECISE = lax.Precision.HIGHEST
MASK_FILL = -1000000000.0


def layer_norm(values, gain_vec):
    centre = jnp.mean(values, axis=-1, keepdims=True)
    centred = values - centre
    spread = jnp.mean(centred * centred, axis=-1, keepdims=True)
    return centred * lax.rsqrt(spread + EPSILON) * gain_vec


def product(left_side, right_side):
    return jnp.dot(left_side, right_side, precision=PRECISE)


def contract_rows(left_side, right_side):
    return lax.dot_general(left_side, right_side, (((0,), (0,)), ((), ())), precision=PRECISE)


def contract_last(left_side, right_side):
    return lax.dot_general(left_side, right_side, (((1,), (1,)), ((), ())), precision=PRECISE)


def attention(queries, keys_in, values_in, key_bias, images, head_width):
    query_len = queries.shape[0] // images
    key_len = keys_in.shape[0] // images
    head_count = queries.shape[1] // head_width
    query_heads = queries.reshape(images, query_len, head_count, head_width)
    key_heads = keys_in.reshape(images, key_len, head_count, head_width)
    value_heads = values_in.reshape(images, key_len, head_count, head_width)
    scores = jnp.einsum("bqhd,bkhd->bhqk", query_heads, key_heads, precision=PRECISE)
    scores = scores / math.sqrt(head_width) + key_bias[:, None, None, :]
    weights = jax.nn.softmax(scores, axis=-1)
    mixture = jnp.einsum("bhqk,bkhd->bqhd", weights, value_heads, precision=PRECISE)
    return mixture.reshape(images * query_len, head_count * head_width)


def attend_local(query_norm, key_norm, w_query, w_key, w_value, key_bias, head_width):
    return attention(
        product(query_norm, w_query),
        product(key_norm, w_key),
        product(key_norm, w_value),
        key_bias,
        key_bias.shape[0],
        head_width,
    )


def expand(norm_full, w_up):
    return jax.nn.gelu(product(norm_full, w_up))


def gather_rows(pieces_in):
    return lax.all_gather(pieces_in, "mp", axis=0, tiled=True)


def branch_sum(source, weight):
    return lax.psum_scatter(product(source, weight), "mp", scatter_dimension=0, tiled=True)


def spread_grad(grad_shard):
    return lax.all_gather(grad_shard, "mp", axis=0, tiled=True)


def collect_grads(pieces_in):
    return lax.psum_scatter(pieces_in, "mp", scatter_dimension=0, tiled=True)


def reduce_branch(weight_grads):
    return lax.psum(weight_grads, "dp")


def norm_backward(source, gain_vec, grad_normed):
    normed, pull_back = jax.vjp(layer_norm, source, gain_vec)
    return pull_back(grad_normed)


def norms_of(query_src, key_src, query_gain, key_gain, crossed):
    if crossed:
        gathered = gather_rows((layer_norm(query_src, query_gain), layer_norm(key_src, key_gain)))
        return (gathered[0], gathered[1])
    gathered = gather_rows((layer_norm(query_src, query_gain),))
    return (gathered[0], gathered[0])


def attend_forward(
    query_src,
    key_src,
    query_gain,
    key_gain,
    w_query,
    w_key,
    w_value,
    w_out,
    key_bias,
    head_width,
    crossed,
):
    query_norm, key_norm = norms_of(query_src, key_src, query_gain, key_gain, crossed)
    mixture = attend_local(query_norm, key_norm, w_query, w_key, w_value, key_bias, head_width)
    return (query_src + branch_sum(mixture, w_out), (query_norm, key_norm))


def attend_backward(
    grad_shard,
    query_src,
    key_src,
    query_gain,
    key_gain,
    w_query,
    w_key,
    w_value,
    w_out,
    key_bias,
    head_width,
    crossed,
):
    query_norm, key_norm = norms_of(query_src, key_src, query_gain, key_gain, crossed)
    if crossed:
        mixture, pull_back = jax.vjp(
            lambda query_in, key_in, query_weight, key_weight, value_weight: attend_local(
                query_in, key_in, query_weight, key_weight, value_weight, key_bias, head_width
            ),
            query_norm,
            key_norm,
            w_query,
            w_key,
            w_value,
        )
    else:
        mixture, pull_back = jax.vjp(
            lambda query_in, query_weight, key_weight, value_weight: attend_local(
                query_in, query_in, query_weight, key_weight, value_weight, key_bias, head_width
            ),
            query_norm,
            w_query,
            w_key,
            w_value,
        )
    grad_full = spread_grad(grad_shard)
    grad_out_weight = contract_rows(mixture, grad_full)
    pulled = pull_back(contract_last(grad_full, w_out))
    if crossed:
        query_part, key_part = collect_grads((pulled[0], pulled[1]))
        grad_query_src, gain_query = norm_backward(query_src, query_gain, query_part)
        grad_key_src, gain_key = norm_backward(key_src, key_gain, key_part)
        weight_grads = reduce_branch((pulled[2], pulled[3], pulled[4], grad_out_weight))
        return (grad_query_src, grad_key_src, (gain_query, gain_key), weight_grads)
    collected = collect_grads((pulled[0],))
    grad_query_src, gain_query = norm_backward(query_src, query_gain, collected[0])
    weight_grads = reduce_branch((pulled[1], pulled[2], pulled[3], grad_out_weight))
    return (grad_query_src, None, (gain_query,), weight_grads)


def expand_forward(stream, gain_vec, w_up, w_down):
    gathered = gather_rows((layer_norm(stream, gain_vec),))
    norm_full = gathered[0]
    return (stream + branch_sum(expand(norm_full, w_up), w_down), norm_full)


def expand_backward(grad_shard, stream, gain_vec, w_up, w_down):
    norm_full = gather_rows((layer_norm(stream, gain_vec),))[0]
    hidden, pull_back = jax.vjp(expand, norm_full, w_up)
    grad_full = spread_grad(grad_shard)
    grad_down = contract_rows(hidden, grad_full)
    grad_norm_full, grad_up = pull_back(contract_last(grad_full, w_down))
    collected = collect_grads((grad_norm_full,))
    grad_stream, grad_gain = norm_backward(stream, gain_vec, collected[0])
    return (grad_shard + grad_stream, grad_gain, reduce_branch((grad_up, grad_down)))


def body(
    interface,
    latents,
    keep_mask,
    read_gain_lat,
    read_gain_int,
    read_query,
    read_keyval,
    read_out,
    read_gain_mlp,
    read_up,
    read_down,
    self_gain_att,
    self_qkv,
    self_out,
    self_gain_mlp,
    self_up,
    self_down,
    write_gain_int,
    write_gain_lat,
    write_query,
    write_keyval,
    write_out,
    write_gain_mlp,
    write_up,
    write_down,
    grad_interface_out,
    grad_latents_out,
):
    images = keep_mask.shape[0]
    shard_rows = interface.shape[0]
    flat_keep = keep_mask.reshape(-1).astype(jnp.float32)
    keep_rows = lax.dynamic_slice_in_dim(
        flat_keep, lax.axis_index("mp") * shard_rows, shard_rows, 0
    )[:, None]
    stream_x0 = interface * keep_rows
    read_bias = jnp.where(keep_mask > 0, 0.0, MASK_FILL).astype(jnp.float32)
    open_bias = jnp.zeros((images, LATENTS), jnp.float32)
    latent_head = D // HEADS
    patch_head = E // HEADS
    stream_z1, read_stored = attend_forward(
        latents,
        stream_x0,
        read_gain_lat,
        read_gain_int,
        read_query,
        read_keyval[0],
        read_keyval[1],
        read_out,
        read_bias,
        latent_head,
        True,
    )
    stream_z, read_mlp_stored = expand_forward(stream_z1, read_gain_mlp, read_up, read_down)
    layer_store = []
    for layer_idx in range(LAYERS):
        attend_input = stream_z
        stream_mid, attend_stored = attend_forward(
            attend_input,
            attend_input,
            self_gain_att[layer_idx],
            self_gain_att[layer_idx],
            self_qkv[layer_idx, 0],
            self_qkv[layer_idx, 1],
            self_qkv[layer_idx, 2],
            self_out[layer_idx],
            open_bias,
            latent_head,
            False,
        )
        stream_z, expand_stored = expand_forward(
            stream_mid, self_gain_mlp[layer_idx], self_up[layer_idx], self_down[layer_idx]
        )
        layer_store.append((attend_input, attend_stored, stream_mid, expand_stored))
    stream_x1, write_stored = attend_forward(
        stream_x0,
        stream_z,
        write_gain_int,
        write_gain_lat,
        write_query,
        write_keyval[0],
        write_keyval[1],
        write_out,
        open_bias,
        patch_head,
        True,
    )
    interface_out, write_mlp_stored = expand_forward(
        stream_x1, write_gain_mlp, write_up, write_down
    )
    grad_x, gain_write_mlp, grads_write_mlp = expand_backward(
        grad_interface_out, stream_x1, write_gain_mlp, write_up, write_down
    )
    grad_query, grad_key, gains_write, grads_write = attend_backward(
        grad_x,
        stream_x0,
        stream_z,
        write_gain_int,
        write_gain_lat,
        write_query,
        write_keyval[0],
        write_keyval[1],
        write_out,
        open_bias,
        patch_head,
        True,
    )
    grad_x = grad_x + grad_query
    grad_z = grad_latents_out + grad_key
    gains_att_list = [None] * LAYERS
    gains_mlp_list = [None] * LAYERS
    grads_att_list = [None] * LAYERS
    grads_mlp_list = [None] * LAYERS
    for layer_idx in reversed(range(LAYERS)):
        attend_input, attend_stored, stream_mid, expand_stored = layer_store[layer_idx]
        grad_z, gain_mlp_layer, grads_mlp_layer = expand_backward(
            grad_z, stream_mid, self_gain_mlp[layer_idx], self_up[layer_idx], self_down[layer_idx]
        )
        grad_self, unused, gains_att_layer, grads_att_layer = attend_backward(
            grad_z,
            attend_input,
            attend_input,
            self_gain_att[layer_idx],
            self_gain_att[layer_idx],
            self_qkv[layer_idx, 0],
            self_qkv[layer_idx, 1],
            self_qkv[layer_idx, 2],
            self_out[layer_idx],
            open_bias,
            latent_head,
            False,
        )
        grad_z = grad_z + grad_self
        gains_att_list[layer_idx] = gains_att_layer[0]
        gains_mlp_list[layer_idx] = gain_mlp_layer
        grads_att_list[layer_idx] = grads_att_layer
        grads_mlp_list[layer_idx] = grads_mlp_layer
    grad_z, gain_read_mlp, grads_read_mlp = expand_backward(
        grad_z, stream_z1, read_gain_mlp, read_up, read_down
    )
    grad_query, grad_key, gains_read, grads_read = attend_backward(
        grad_z,
        latents,
        stream_x0,
        read_gain_lat,
        read_gain_int,
        read_query,
        read_keyval[0],
        read_keyval[1],
        read_out,
        read_bias,
        latent_head,
        True,
    )
    grad_z = grad_z + grad_query
    grad_x = grad_x + grad_key
    grad_interface = grad_x * keep_rows
    summed_gains = lax.psum(
        (
            gains_read[0],
            gains_read[1],
            gain_read_mlp,
            jnp.stack(gains_att_list),
            jnp.stack(gains_mlp_list),
            gains_write[0],
            gains_write[1],
            gain_write_mlp,
        ),
        ("dp", "mp"),
    )
    self_qkv_grad = jnp.stack(
        [jnp.stack([entry[0], entry[1], entry[2]]) for entry in grads_att_list]
    )
    self_out_grad = jnp.stack([entry[3] for entry in grads_att_list])
    self_up_grad = jnp.stack([entry[0] for entry in grads_mlp_list])
    self_down_grad = jnp.stack([entry[1] for entry in grads_mlp_list])
    weight_tuple = (
        grads_read[0],
        jnp.stack([grads_read[1], grads_read[2]]),
        grads_read[3],
        grads_read_mlp[0],
        grads_read_mlp[1],
        self_qkv_grad,
        self_out_grad,
        self_up_grad,
        self_down_grad,
        grads_write[0],
        jnp.stack([grads_write[1], grads_write[2]]),
        grads_write[3],
        grads_write_mlp[0],
        grads_write_mlp[1],
    )
    return (
        interface_out,
        stream_z,
        grad_interface,
        grad_z,
        summed_gains[0],
        summed_gains[1],
        weight_tuple[0],
        weight_tuple[1],
        weight_tuple[2],
        summed_gains[2],
        weight_tuple[3],
        weight_tuple[4],
        summed_gains[3],
        weight_tuple[5],
        weight_tuple[6],
        summed_gains[4],
        weight_tuple[7],
        weight_tuple[8],
        summed_gains[5],
        summed_gains[6],
        weight_tuple[9],
        weight_tuple[10],
        weight_tuple[11],
        summed_gains[7],
        weight_tuple[12],
        weight_tuple[13],
    )


def solution(mesh):
    in_specs = (
        P(("dp", "mp"), None),
        P(("dp", "mp"), None),
        P("dp", None),
        P(),
        P(),
        P(None, "mp"),
        P(None, None, "mp"),
        P("mp", None),
        P(),
        P(None, "mp"),
        P("mp", None),
        P(),
        P(None, None, None, "mp"),
        P(None, "mp", None),
        P(),
        P(None, None, "mp"),
        P(None, "mp", None),
        P(),
        P(),
        P(None, "mp"),
        P(None, None, "mp"),
        P("mp", None),
        P(),
        P(None, "mp"),
        P("mp", None),
        P(("dp", "mp"), None),
        P(("dp", "mp"), None),
    )
    out_specs = (
        P(("dp", "mp"), None),
        P(("dp", "mp"), None),
        P(("dp", "mp"), None),
        P(("dp", "mp"), None),
        P(),
        P(),
        P(None, "mp"),
        P(None, None, "mp"),
        P("mp", None),
        P(),
        P(None, "mp"),
        P("mp", None),
        P(),
        P(None, None, None, "mp"),
        P(None, "mp", None),
        P(),
        P(None, None, "mp"),
        P(None, "mp", None),
        P(),
        P(),
        P(None, "mp"),
        P(None, None, "mp"),
        P("mp", None),
        P(),
        P(None, "mp"),
        P("mp", None),
    )
    return jax.shard_map(body, mesh=mesh, in_specs=in_specs, out_specs=out_specs, check_vma=False)
```

profile of v0, /device:TPU:0, one launch (start us, length us, event | category | flops | bytes accessed | tf_op | source)
XLA Modules:
  0.0 2203.9 jit_solution(14452684715133826007)
XLA Ops:
  19.0 10.0 all_gather.65
  30.8 8.7 all-gather.6.cloned.1.call-done
  53.9 22.6 %reduce-scatter.19.cloned.1.call-done = f32[32,1024]{1,0:T(8,128)} async-done(((f32[128,1024]{1,0:T(8,128)}), f32[32,1024]{1,0:T(8,128)}) %reduce-scatter.19.cloned.1.call-update) | async-done | bytes 131088 | tf_op jit(solution)/shard_map/reduce_scatter | solution.py:70
  78.8 7.1 all_gather.66
  95.0 5.5 slice_bitcast_fusion
  108.2 8.9 reduce-scatter.21.cloned.1.call-done
  119.2 6.9 all_gather.67
  134.0 21.3 reduce-scatter.23.cloned.1.call-done
  157.2 7.0 all_gather.68
  169.8 5.5 fusion.10
  183.0 14.5 reduce-scatter.25.cloned.1.call-done
  199.6 6.9 all_gather.69
  214.3 21.4 reduce-scatter.27.cloned.1.call-done
  237.6 7.2 all_gather.70
  250.7 5.5 fusion.2
  267.3 18.1 reduce-scatter.29.cloned.1.call-done
  287.4 6.8 all_gather.71
  305.2 31.3 %reduce-scatter.31.cloned.1.call-done = f32[256,512]{1,0:T(8,128)} async-done(((f32[1024,512]{1,0:T(8,128)}), f32[256,512]{1,0:T(8,128)}) %reduce-scatter.31.cloned.1.call-update) | async-done | bytes 524304 | tf_op jit(solution)/shard_map/reduce_scatter | solution.py:70
  340.5 20.1 all-gather.12.cloned.1.call-done
  360.6 6.6 fusion.207
  367.2 18.2 all-gather.10.cloned.1.call-done
  385.5 9.6 fusion.29
  402.4 6.9 fusion.54
  409.4 23.4 %reduce-scatter.35.cloned.1.call-done = f32[256,512]{1,0:T(8,128)} async-done(((f32[1024,512]{1,0:T(8,128)}), f32[256,512]{1,0:T(8,128)}) %reduce-scatter.35.cloned.1.call-update) | async-done | bytes 524304 | tf_op jit(solution)/shard_map/reduce_scatter | solution.py:78
  435.9 31.4 %reduce-scatter.33.cloned.1.call-done = f32[256,512]{1,0:T(8,128)} async-done(((f32[1024,512]{1,0:T(8,128)}), f32[256,512]{1,0:T(8,128)}) %reduce-scatter.33.cloned.1.call-update) | async-done | bytes 524304 | tf_op jit(solution)/shard_map/reduce_scatter | solution.py:70
  470.5 22.7 %all-gather.14.cloned.1.call-done = f32[1024,512]{1,0:T(8,128)} async-done(((f32[256,512]{1,0:T(8,128)}), f32[1024,512]{1,0:T(8,128)}) %all-gather.14.cloned.1.call-update) | async-done | bytes 2097168 | tf_op jit(solution)/shard_map/all_gather | solution.py:74
  508.6 21.8 reduce-scatter.39.cloned.1.call-done
  533.9 7.2 all_gather.76
  541.0 6.9 fusion.75
  548.7 7.3 fusion.4
  559.4 18.9 reduce-scatter.41.cloned.1.call-done
  581.2 7.1 all_gather.77
  600.2 22.1 %reduce-scatter.43.cloned.1.call-done = f32[32,1024]{1,0:T(8,128)} async-done(((f32[128,1024]{1,0:T(8,128)}), f32[32,1024]{1,0:T(8,128)}) %reduce-scatter.43.cloned.1.call-update) | async-done | bytes 131088 | tf_op jit(solution)/shard_map/reduce_scatter | solution.py:78
  625.9 7.0 all_gather.78
  632.9 6.9 fusion.69
  640.6 7.4 fusion.12
  648.1 22.1 %reduce-scatter.45.cloned.1.call-done = f32[32,1024]{1,0:T(8,128)} async-done(((f32[128,1024]{1,0:T(8,128)}), f32[32,1024]{1,0:T(8,128)}) %reduce-scatter.45.cloned.1.call-update) | async-done | bytes 131088 | tf_op jit(solution)/shard_map/reduce_scatter | solution.py:78
  673.2 7.2 all_gather.79
  692.2 22.2 %reduce-scatter.47.cloned.1.call-done = f32[32,1024]{1,0:T(8,128)} async-done(((f32[128,1024]{1,0:T(8,128)}), f32[32,1024]{1,0:T(8,128)}) %reduce-scatter.47.cloned.1.call-update) | async-done | bytes 131088 | tf_op jit(solution)/shard_map/reduce_scatter | solution.py:78
  717.2 7.2 all_gather.80
  724.4 6.8 fusion.213
  738.1 21.5 reduce-scatter.49.cloned.1.call-done
  763.3 7.0 all_gather.81
  789.2 6.9 fusion.222
  868.4 5.5 fusion.178
  893.9 47.7 %all-reduce = (f32[1024]{0:T(1024)}, f32[512]{0:T(512)}, f32[1024]{0:T(1024)}, f32[2,1024]{1,0:T(2,128)}, f32[2,1024]{1,0:T(2,128)}, /*index=5*/f32[512]{0:T(512)}, f32[1024]{0:T(1024)}, f32[512]{0:T(512)}) all-reduce(f32[1024]{0:T(1024)S(1)} %get-tuple-element.48, ...), channel_id=1, replica_groups=mesh['dp'=8,'mp'=4] {'dp','mp'}, use_global_device_ids=true, to_apply=%region_69.70 | all-reduce | flops 8704 | bytes 69632 | tf_op jit(solution)/shard_map/psum | solution.py:341
  942.8 1218.9 %all-reduce.4.cloned.1.call-done = (f32[1024,256]{1,0:T(8,128)}, f32[1,512,256]{2,1,0:T(8,128)}, f32[1,512,256]{2,1,0:T(8,128)}, f32[256,1024]{1,0:T(8,128)}, f3...) async-done(((f32[1024,256]{1,0:T(8,128)}, ...) | async-done | bytes 40370192 | tf_op jit(solution)/shard_map/psum | solution.py:82
  2177.7 6.8 pad_maximum_fusion
  (814 shorter events, 339.5 us)
Async XLA Ops:
  7.2 378.3 %copy-start = (f32[512,512]{1,0:T(8,128)S(1)}, f32[512,512]{1,0:T(8,128)}, u32[]{:S(2)}) copy-start(f32[512,512]{1,0:T(8,128)} %param.50) | copy-start | bytes 3145732
  7.2 32.3 %all-gather.6.cloned.1.call-start = ((), (), s32[]{:S(2)}) async-start(), calls=%async_computation.18 | async-start | bytes 2621440 | tf_op jit(solution)/shard_map/all_gather | solution.py:66
  12.9 63.6 %reduce-scatter.19.cloned.1.call-start = ((), (), s32[]{:S(2)}) async-start(), calls=%async_computation.19 | async-start | bytes 655360 | tf_op jit(solution)/shard_map/reduce_scatter | solution.py:70
  53.8 63.3 %reduce-scatter.21.cloned.1.call-start = ((), (), s32[]{:S(2)}) async-start(), calls=%async_computation.20 | async-start | bytes 655360 | tf_op jit(solution)/shard_map/reduce_scatter | solution.py:70
  95.0 60.3 %reduce-scatter.23.cloned.1.call-start = ((), (), s32[]{:S(2)}) async-start(), calls=%async_computation.21 | async-start | bytes 655360 | tf_op jit(solution)/shard_map/reduce_scatter | solution.py:70
  108.2 91.2 %copy-start.183 = (f32[1,1024]{1,0:T(1,128)}, f32[1,1024]{1,0:T(1,128)S(1)}, u32[]{:S(2)}) copy-start(f32[1,1024]{1,0:T(1,128)S(1)} %get-tuple-element.131) | copy-start | bytes 12292
  133.2 64.3 %reduce-scatter.25.cloned.1.call-start = ((), (), s32[]{:S(2)}) async-start(), calls=%async_computation.22 | async-start | bytes 655360 | tf_op jit(solution)/shard_map/reduce_scatter | solution.py:70
  134.0 35.0 %copy-start.185 = (f32[1,1024]{1,0:T(1,128)}, f32[1,1024]{1,0:T(1,128)S(1)}, u32[]{:S(2)}) copy-start(f32[1,1024]{1,0:T(1,128)S(1)} %get-tuple-element.130) | copy-start | bytes 12292
  134.0 103.5 %copy-start.187 = (f32[1,1024]{1,0:T(1,128)}, f32[1,1024]{1,0:T(1,128)S(1)}, u32[]{:S(2)}) copy-start(f32[1,1024]{1,0:T(1,128)S(1)} %get-tuple-element.129) | copy-start | bytes 12292
  175.3 60.3 %reduce-scatter.27.cloned.1.call-start = ((), (), s32[]{:S(2)}) async-start(), calls=%async_computation.23 | async-start | bytes 655360 | tf_op jit(solution)/shard_map/reduce_scatter | solution.py:70
  213.5 49.2 %all-gather.8.cloned.1.call-start = ((), (), s32[]{:S(2)}) async-start(), calls=%async_computation.25 | async-start | bytes 2621440 | tf_op jit(solution)/shard_map/all_gather | solution.py:66
  214.2 71.2 %reduce-scatter.29.cloned.1.call-start = ((), (), s32[]{:S(2)}) async-start(), calls=%async_computation.24 | async-start | bytes 655360 | tf_op jit(solution)/shard_map/reduce_scatter | solution.py:70
  256.3 80.2 %reduce-scatter.31.cloned.1.call-start = ((), (), s32[]{:S(2)}) async-start(), calls=%async_computation.26 | async-start | bytes 2621440 | tf_op jit(solution)/shard_map/reduce_scatter | solution.py:70
  304.6 56.0 %all-gather.12.cloned.1.call-start = ((), (), s32[]{:S(2)}) async-start(), calls=%async_computation.29 | async-start | bytes 2621440 | tf_op jit(solution)/shard_map/all_gather | solution.py:74
  305.2 80.3 %all-gather.10.cloned.1.call-start = ((), (), s32[]{:S(2)}) async-start(), calls=%async_computation.27 | async-start | bytes 2621440 | tf_op jit(solution)/shard_map/all_gather | solution.py:66
  340.3 92.5 %reduce-scatter.35.cloned.1.call-start = ((), (), s32[]{:S(2)}) async-start(), calls=%async_computation.30 | async-start | bytes 2621440 | tf_op jit(solution)/shard_map/reduce_scatter | solution.py:78
  401.2 66.1 %reduce-scatter.33.cloned.1.call-start = ((), (), s32[]{:S(2)}) async-start(), calls=%async_computation.28 | async-start | bytes 2621440 | tf_op jit(solution)/shard_map/reduce_scatter | solution.py:70
  409.3 60.2 %copy-start.111 = (f32[256,512]{1,0:T(8,128)S(1)}, f32[256,512]{1,0:T(8,128)}, u32[]{:S(2)}) copy-start(f32[256,512]{1,0:T(8,128)} %param.52) | copy-start | bytes 1572868
  409.3 83.9 %all-gather.14.cloned.1.call-start = ((), (), s32[]{:S(2)}) async-start(), calls=%async_computation.31 | async-start | bytes 2621440 | tf_op jit(solution)/shard_map/all_gather | solution.py:74
  470.5 59.9 %reduce-scatter.39.cloned.1.call-start = ((), (), s32[]{:S(2)}) async-start(), calls=%async_computation.33 | async-start | bytes 655360 | tf_op jit(solution)/shard_map/reduce_scatter | solution.py:78
  507.0 34.0 %copy-start.34 = (f32[128,1024]{1,0:T(8,128)S(1)}, f32[128,1024]{1,0:T(8,128)}, u32[]{:S(2)}) copy-start(f32[128,1024]{1,0:T(8,128)} %copy-done.33) | copy-start | bytes 1572868
  508.5 69.7 %reduce-scatter.41.cloned.1.call-start = ((), (), s32[]{:S(2)}) async-start(), calls=%async_computation.34 | async-start | bytes 655360 | tf_op jit(solution)/shard_map/reduce_scatter | solution.py:78
  556.1 66.2 %reduce-scatter.43.cloned.1.call-start = ((), (), s32[]{:S(2)}) async-start(), calls=%async_computation.35 | async-start | bytes 655360 | tf_op jit(solution)/shard_map/reduce_scatter | solution.py:78
  559.3 30.0 %copy-start.107 = (f32[4,128,128]{1,2,0:T(8,128)S(1)}, f32[4,128,128]{1,2,0:T(8,128)}, u32[]{:S(2)}) copy-start(f32[4,128,128]{1,2,0:T(8,128)} %copy-done.106) | copy-start | bytes 786436
  559.3 30.0 %copy-start.207 = (f32[4,128]{1,0:T(4,128)S(1)}, f32[4,128]{1,0:T(4,128)}, u32[]{:S(2)}) copy-start(f32[4,128]{1,0:T(4,128)} %copy-done.206) | copy-start | bytes 6148
  594.3 29.7 %copy-start.265 = (f32[32]{0:T(128)S(1)}, f32[32]{0:T(128)}, u32[]{:S(2)}) copy-start(f32[32]{0:T(128)} %copy-done.264) | copy-start | bytes 388
  596.8 36.0 %copy-start.31 = (f32[128,1024]{1,0:T(8,128)S(1)}, f32[128,1024]{1,0:T(8,128)}, u32[]{:S(2)}) copy-start(f32[128,1024]{1,0:T(8,128)} %copy-done.30) | copy-start | bytes 1572868
  600.2 70.0 %reduce-scatter.45.cloned.1.call-start = ((), (), s32[]{:S(2)}) async-start(), calls=%async_computation.36 | async-start | bytes 655360 | tf_op jit(solution)/shard_map/reduce_scatter | solution.py:78
  640.5 29.7 %copy-start.54 = (f32[32,1024]{1,0:T(8,128)S(1)}, f32[32,1024]{1,0:T(8,128)}, u32[]{:S(2)}) copy-start(f32[32,1024]{1,0:T(8,128)} %copy-done.53) | copy-start | bytes 393220
  640.5 29.7 %copy-start.186 = (f32[1,1024]{1,0:T(1,128)S(1)}, f32[1,1024]{1,0:T(1,128)}, u32[]{:S(2)}) copy-start(f32[1,1024]{1,0:T(1,128)} %copy-done.185) | copy-start | bytes 12292
  640.5 29.7 %copy-start.230 = (f32[32]{0:T(128)S(1)}, f32[32]{0:T(128)}, u32[]{:S(2)}) copy-start(f32[32]{0:T(128)} %copy-done.229) | copy-start | bytes 388
  640.5 29.7 %copy-start.250 = (f32[32]{0:T(128)S(1)}, f32[32]{0:T(128)}, u32[]{:S(2)}) copy-start(f32[32]{0:T(128)} %copy-done.249) | copy-start | bytes 388
  640.5 31.4 %copy-start.263 = (f32[32]{0:T(128)S(1)}, f32[32]{0:T(128)}, u32[]{:S(2)}) copy-start(f32[32]{0:T(128)} %copy-done.262) | copy-start | bytes 388
  640.5 32.5 %copy-start.118 = (f32[32,1024]{1,0:T(8,128)S(1)}, f32[32,1024]{1,0:T(8,128)}, u32[]{:S(2)}) copy-start(f32[32,1024]{1,0:T(8,128)} %copy-done.117) | copy-start | bytes 393220
  648.0 33.4 %copy-start.105 = (f32[4,128,128]{1,2,0:T(8,128)S(1)}, f32[4,128,128]{1,2,0:T(8,128)}, u32[]{:S(2)}) copy-start(f32[4,128,128]{1,2,0:T(8,128)} %copy-done.104) | copy-start | bytes 786436
  648.0 33.4 %copy-start.205 = (f32[4,128]{1,0:T(4,128)S(1)}, f32[4,128]{1,0:T(4,128)}, u32[]{:S(2)}) copy-start(f32[4,128]{1,0:T(4,128)} %copy-done.204) | copy-start | bytes 6148
  648.0 66.4 %reduce-scatter.47.cloned.1.call-start = ((), (), s32[]{:S(2)}) async-start(), calls=%async_computation.37 | async-start | bytes 655360 | tf_op jit(solution)/shard_map/reduce_scatter | solution.py:78
  686.3 29.7 %copy-start.261 = (f32[32]{0:T(128)S(1)}, f32[32]{0:T(128)}, u32[]{:S(2)}) copy-start(f32[32]{0:T(128)} %copy-done.260) | copy-start | bytes 388
  692.1 67.5 %reduce-scatter.49.cloned.1.call-start = ((), (), s32[]{:S(2)}) async-start(), calls=%async_computation.38 | async-start | bytes 655360 | tf_op jit(solution)/shard_map/reduce_scatter | solution.py:78
  737.4 35.2 %copy-start.180 = (f32[1,1024]{1,0:T(1,128)S(1)}, f32[1,1024]{1,0:T(1,128)}, u32[]{:S(2)}) copy-start(f32[1,1024]{1,0:T(1,128)} %copy-done.179) | copy-start | bytes 12292
  737.4 35.3 %copy-start.200 = (f32[4,128]{1,0:T(4,128)S(1)}, f32[4,128]{1,0:T(4,128)}, u32[]{:S(2)}) copy-start(f32[4,128]{1,0:T(4,128)} %copy-done.199) | copy-start | bytes 6148
  737.5 149.8 %reduce-scatter.53.cloned.1.call-start = ((), (), s32[]{:S(2)}) async-start(), calls=%async_computation.40 | async-start | bytes 655360 | tf_op jit(solution)/shard_map/reduce_scatter | solution.py:78
  781.8 108.6 %reduce-scatter.37.cloned.1.call-start = ((), (), s32[]{:S(2)}) async-start(), calls=%async_computation.32 | async-start | bytes 2621440 | tf_op jit(solution)/shard_map/reduce_scatter | solution.py:78
  788.9 101.4 %reduce-scatter.51.cloned.1.call-start = ((), (), s32[]{:S(2)}) async-start(), calls=%async_computation.39 | async-start | bytes 2621440 | tf_op jit(solution)/shard_map/reduce_scatter | solution.py:78
  815.9 1345.8 %all-reduce.4.cloned.1.call-start = ((), (), s32[]{:S(2)}) async-start(), calls=%async_computation.41 | async-start | bytes 80740352 | tf_op jit(solution)/shard_map/psum | solution.py:82
  887.2 54.4 %copy-start.71 = (f32[256,512]{1,0:T(8,128)S(1)}, f32[256,512]{1,0:T(8,128)}, u32[]{:S(2)}) copy-start(f32[256,512]{1,0:T(8,128)} %add_add_fusion.3) | copy-start | bytes 1572868
  890.3 51.3 %copy-start.59 = (f32[256,512]{1,0:T(8,128)S(1)}, f32[256,512]{1,0:T(8,128)}, u32[]{:S(2)}) copy-start(f32[256,512]{1,0:T(8,128)} %reduce-scatter.37.cloned.1.call-done) | copy-start | bytes 1572868
  890.4 51.2 %copy-start.60 = (f32[256,512]{1,0:T(8,128)S(1)}, f32[256,512]{1,0:T(8,128)}, u32[]{:S(2)}) copy-start(f32[256,512]{1,0:T(8,128)} %reduce-scatter.51.cloned.1.call-done) | copy-start | bytes 1572868
  (247 other events, 1711.8 us)
Sparse Core Ops, SparseCore 0:
  13.0 26.4 all-gather.5
  54.0 22.4 reduce-scatter.18
  95.1 22.0 reduce-scatter.20
  133.3 21.9 reduce-scatter.22
  175.4 22.0 reduce-scatter.24
  213.6 22.0 reduce-scatter.26
  237.9 22.5 all-gather.7
  263.7 21.6 reduce-scatter.28
  304.7 31.7 reduce-scatter.30
  338.0 22.5 all-gather.11
  362.8 22.5 all-gather.9
  401.3 31.4 reduce-scatter.34
  435.9 31.3 reduce-scatter.32
  470.6 22.5 all-gather.13
  508.6 21.6 reduce-scatter.38
  556.2 22.0 reduce-scatter.40
  600.3 22.0 reduce-scatter.42
  648.1 22.0 reduce-scatter.44
  692.3 22.0 reduce-scatter.46
  737.6 22.0 reduce-scatter.48
  781.9 22.0 reduce-scatter.52
  806.5 31.4 reduce-scatter.36
  841.2 31.3 reduce-scatter.50
  886.7 1274.9 all-reduce.3
where the time goes:
time: 2220 us; the launch traced here: 2200 us
  waiting for transfers between devices  1610 us (73%)
  matrix products  284 us (13%)
  blocking collectives  142 us (6%)
  local copies, waits for them, and re-layouts  76.6 us (3%)
  other arithmetic  69.8 us (3%)
    psum x1, waiting for transfers between devices, reduce_branch(): return lax.psum(weight_grads, 'dp')  1220 us
    dot_general x56, matrix products, product(): return jnp.dot(left_side, right_side, precision=PRECISE)  186 us
    reduce_scatter x8, waiting for transfers between devices, branch_sum(): lax.psum_scatter(product(source, weight), 'mp', scatter_dimension=0, tile...  169 us
    reduce_scatter x10, waiting for transfers between devices, collect_grads(): return lax.psum_scatter(pieces_in, 'mp', scatter_dimension=0, tiled=True)  152 us
    all_gather x7, blocking collectives, gather_rows(): return lax.all_gather(pieces_in, 'mp', axis=0, tiled=True)  51.9 us
    psum x1, blocking collectives, body(): lax.psum((gains_read[0], gains_read[1], gain_read_mlp, jnp.stack(gains_at...  47.7 us
  transfers between devices with their start and end apart: 24, of which 20 were waited for; matrix products, arithmetic and copies ran while one was open for 8% of the time, Pallas kernels for 0%

commit v1 on v0

--- a/solution.py
+++ b/solution.py
@@ -338,19 +338,18 @@
     grad_z = grad_z + grad_query
     grad_x = grad_x + grad_key
     grad_interface = grad_x * keep_rows
-    summed_gains = lax.psum(
-        (
-            gains_read[0],
-            gains_read[1],
-            gain_read_mlp,
-            jnp.stack(gains_att_list),
-            jnp.stack(gains_mlp_list),
-            gains_write[0],
-            gains_write[1],
-            gain_write_mlp,
-        ),
-        ("dp", "mp"),
-    )
+    shard_in = (
+        gains_read[0],
+        gains_read[1],
+        gain_read_mlp,
+        jnp.stack(gains_att_list),
+        jnp.stack(gains_mlp_list),
+        gains_write[0],
+        gains_write[1],
+        gain_write_mlp,
+    )
+    y_new = lax.psum(shard_in, "mp")
+    summed_gains = lax.psum(y_new, "dp")
     self_qkv_grad = jnp.stack(
         [jnp.stack([entry[0], entry[1], entry[2]]) for entry in grads_att_list]
     )

time: 2220 us -> 2220 us (level)
    psum x1 -> x2, blocking collectives: 47.7 us -> 53.3 us  [the longest x1 41.3 us: body(): summed_gains = lax.psum(y_new, 'dp')]
where the time goes in v1:
time: 2220 us; the launch traced here: 2200 us
  waiting for transfers between devices  1610 us (73%)
  matrix products  284 us (13%)
  blocking collectives  148 us (7%)
  local copies, waits for them, and re-layouts  76.5 us (3%)
  other arithmetic  69.7 us (3%)
    psum x1, waiting for transfers between devices, reduce_branch(): return lax.psum(weight_grads, 'dp')  1210 us
    dot_general x56, matrix products, product(): return jnp.dot(left_side, right_side, precision=PRECISE)  186 us
    reduce_scatter x8, waiting for transfers between devices, branch_sum(): lax.psum_scatter(product(source, weight), 'mp', scatter_dimension=0, tile...  170 us
    reduce_scatter x10, waiting for transfers between devices, collect_grads(): return lax.psum_scatter(pieces_in, 'mp', scatter_dimension=0, tiled=True)  152 us
    all_gather x7, blocking collectives, gather_rows(): return lax.all_gather(pieces_in, 'mp', axis=0, tiled=True)  51.8 us
  transfers between devices with their start and end apart: 24, of which 20 were waited for; matrix products, arithmetic and copies ran while one was open for 8% of the time, Pallas kernels for 0%

profile of v1, /device:TPU:0, one launch (start us, length us, event | category | flops | bytes accessed | tf_op | source)
XLA Modules:
  0.0 2203.9 jit_solution(16757406105640829327)
XLA Ops:
  18.9 9.9 all_gather.65
  30.7 8.8 all-gather.6.cloned.1.call-done
  53.8 22.6 %reduce-scatter.19.cloned.1.call-done = f32[32,1024]{1,0:T(8,128)} async-done(((f32[128,1024]{1,0:T(8,128)}), f32[32,1024]{1,0:T(8,128)}) %reduce-scatter.19.cloned.1.call-update) | async-done | bytes 131088 | tf_op jit(solution)/shard_map/reduce_scatter | solution.py:70
  78.7 7.1 all_gather.66
  94.9 5.5 slice_bitcast_fusion
  108.1 8.9 reduce-scatter.21.cloned.1.call-done
  119.1 6.9 all_gather.67
  133.8 21.3 reduce-scatter.23.cloned.1.call-done
  157.1 7.0 all_gather.68
  182.8 14.5 reduce-scatter.25.cloned.1.call-done
  199.5 6.9 all_gather.69
  214.2 21.4 reduce-scatter.27.cloned.1.call-done
  237.5 7.2 all_gather.70
  250.6 5.5 fusion.2
  267.2 18.1 reduce-scatter.29.cloned.1.call-done
  287.4 6.8 all_gather.71
  305.2 31.3 %reduce-scatter.31.cloned.1.call-done = f32[256,512]{1,0:T(8,128)} async-done(((f32[1024,512]{1,0:T(8,128)}), f32[256,512]{1,0:T(8,128)}) %reduce-scatter.31.cloned.1.call-update) | async-done | bytes 524304 | tf_op jit(solution)/shard_map/reduce_scatter | solution.py:70
  340.5 20.1 all-gather.12.cloned.1.call-done
  360.6 6.6 fusion.207
  367.2 18.2 all-gather.10.cloned.1.call-done
  385.4 9.6 fusion.29
  402.3 6.9 fusion.54
  409.3 23.4 %reduce-scatter.35.cloned.1.call-done = f32[256,512]{1,0:T(8,128)} async-done(((f32[1024,512]{1,0:T(8,128)}), f32[256,512]{1,0:T(8,128)}) %reduce-scatter.35.cloned.1.call-update) | async-done | bytes 524304 | tf_op jit(solution)/shard_map/reduce_scatter | solution.py:78
  435.8 31.4 %reduce-scatter.33.cloned.1.call-done = f32[256,512]{1,0:T(8,128)} async-done(((f32[1024,512]{1,0:T(8,128)}), f32[256,512]{1,0:T(8,128)}) %reduce-scatter.33.cloned.1.call-update) | async-done | bytes 524304 | tf_op jit(solution)/shard_map/reduce_scatter | solution.py:70
  470.5 22.7 %all-gather.14.cloned.1.call-done = f32[1024,512]{1,0:T(8,128)} async-done(((f32[256,512]{1,0:T(8,128)}), f32[1024,512]{1,0:T(8,128)}) %all-gather.14.cloned.1.call-update) | async-done | bytes 2097168 | tf_op jit(solution)/shard_map/all_gather | solution.py:74
  508.5 21.8 reduce-scatter.39.cloned.1.call-done
  533.8 7.2 all_gather.76
  541.0 6.9 fusion.75
  548.6 7.3 fusion.4
  559.3 18.9 reduce-scatter.41.cloned.1.call-done
  581.2 7.1 all_gather.77
  600.2 22.2 %reduce-scatter.43.cloned.1.call-done = f32[32,1024]{1,0:T(8,128)} async-done(((f32[128,1024]{1,0:T(8,128)}), f32[32,1024]{1,0:T(8,128)}) %reduce-scatter.43.cloned.1.call-update) | async-done | bytes 131088 | tf_op jit(solution)/shard_map/reduce_scatter | solution.py:78
  625.8 7.0 all_gather.78
  632.8 6.9 fusion.69
  640.5 7.4 fusion.12
  648.0 22.1 %reduce-scatter.45.cloned.1.call-done = f32[32,1024]{1,0:T(8,128)} async-done(((f32[128,1024]{1,0:T(8,128)}), f32[32,1024]{1,0:T(8,128)}) %reduce-scatter.45.cloned.1.call-update) | async-done | bytes 131088 | tf_op jit(solution)/shard_map/reduce_scatter | solution.py:78
  673.1 7.1 all_gather.79
  692.1 22.2 %reduce-scatter.47.cloned.1.call-done = f32[32,1024]{1,0:T(8,128)} async-done(((f32[128,1024]{1,0:T(8,128)}), f32[32,1024]{1,0:T(8,128)}) %reduce-scatter.47.cloned.1.call-update) | async-done | bytes 131088 | tf_op jit(solution)/shard_map/reduce_scatter | solution.py:78
  717.1 7.2 all_gather.80
  724.4 6.8 fusion.213
  738.1 21.5 reduce-scatter.49.cloned.1.call-done
  763.2 6.9 all_gather.81
  789.0 6.9 fusion.222
  868.2 5.5 fusion.178
  893.7 12.0 all-reduce.2
  905.7 41.3 %all-reduce = (f32[1024]{0:T(1024)}, f32[512]{0:T(512)}, f32[1024]{0:T(1024)}, f32[2,1024]{1,0:T(2,128)}, f32[2,1024]{1,0:T(2,128)}, /*index=5*/f32[512]{0:T(512)}, f32[1024]{0:T(1024)}, f32[512]{0:T(512)}) all-reduce(f32[1024]{0:T(1024)S(1)} %get-tuple-element.82, ...), channel_id=1, replica_groups=mesh['dp'=8,'mp'=4] {'dp'}, use_global_device_ids=true, to_apply=%region_70.71 | all-reduce | flops 8704 | bytes 69632 | tf_op jit(solution)/shard_map/psum | solution.py:352
  948.1 1213.6 %all-reduce.5.cloned.1.call-done = (f32[1024,256]{1,0:T(8,128)}, f32[1,512,256]{2,1,0:T(8,128)}, f32[1,512,256]{2,1,0:T(8,128)}, f32[256,1024]{1,0:T(8,128)}, f3...) async-done(((f32[1024,256]{1,0:T(8,128)}, ...) | async-done | bytes 40370192 | tf_op jit(solution)/shard_map/psum | solution.py:82
  2177.8 6.8 pad_maximum_fusion
  (815 shorter events, 344.7 us)
Async XLA Ops:
  7.2 378.2 %copy-start = (f32[512,512]{1,0:T(8,128)S(1)}, f32[512,512]{1,0:T(8,128)}, u32[]{:S(2)}) copy-start(f32[512,512]{1,0:T(8,128)} %param.50) | copy-start | bytes 3145732
  7.2 32.2 %all-gather.6.cloned.1.call-start = ((), (), s32[]{:S(2)}) async-start(), calls=%async_computation.18 | async-start | bytes 2621440 | tf_op jit(solution)/shard_map/all_gather | solution.py:66
  12.9 63.5 %reduce-scatter.19.cloned.1.call-start = ((), (), s32[]{:S(2)}) async-start(), calls=%async_computation.19 | async-start | bytes 655360 | tf_op jit(solution)/shard_map/reduce_scatter | solution.py:70
  53.8 63.2 %reduce-scatter.21.cloned.1.call-start = ((), (), s32[]{:S(2)}) async-start(), calls=%async_computation.20 | async-start | bytes 655360 | tf_op jit(solution)/shard_map/reduce_scatter | solution.py:70
  94.8 60.3 %reduce-scatter.23.cloned.1.call-start = ((), (), s32[]{:S(2)}) async-start(), calls=%async_computation.21 | async-start | bytes 655360 | tf_op jit(solution)/shard_map/reduce_scatter | solution.py:70
  108.0 91.3 %copy-start.183 = (f32[1,1024]{1,0:T(1,128)}, f32[1,1024]{1,0:T(1,128)S(1)}, u32[]{:S(2)}) copy-start(f32[1,1024]{1,0:T(1,128)S(1)} %get-tuple-element.139) | copy-start | bytes 12292
  132.9 64.4 %reduce-scatter.25.cloned.1.call-start = ((), (), s32[]{:S(2)}) async-start(), calls=%async_computation.22 | async-start | bytes 655360 | tf_op jit(solution)/shard_map/reduce_scatter | solution.py:70
  133.8 35.0 %copy-start.185 = (f32[1,1024]{1,0:T(1,128)}, f32[1,1024]{1,0:T(1,128)S(1)}, u32[]{:S(2)}) copy-start(f32[1,1024]{1,0:T(1,128)S(1)} %get-tuple-element.138) | copy-start | bytes 12292
  133.8 103.6 %copy-start.187 = (f32[1,1024]{1,0:T(1,128)}, f32[1,1024]{1,0:T(1,128)S(1)}, u32[]{:S(2)}) copy-start(f32[1,1024]{1,0:T(1,128)S(1)} %get-tuple-element.137) | copy-start | bytes 12292
  175.1 60.4 %reduce-scatter.27.cloned.1.call-start = ((), (), s32[]{:S(2)}) async-start(), calls=%async_computation.23 | async-start | bytes 655360 | tf_op jit(solution)/shard_map/reduce_scatter | solution.py:70
  213.4 49.2 %all-gather.8.cloned.1.call-start = ((), (), s32[]{:S(2)}) async-start(), calls=%async_computation.25 | async-start | bytes 2621440 | tf_op jit(solution)/shard_map/all_gather | solution.py:66
  214.1 71.2 %reduce-scatter.29.cloned.1.call-start = ((), (), s32[]{:S(2)}) async-start(), calls=%async_computation.24 | async-start | bytes 655360 | tf_op jit(solution)/shard_map/reduce_scatter | solution.py:70
  256.2 80.3 %reduce-scatter.31.cloned.1.call-start = ((), (), s32[]{:S(2)}) async-start(), calls=%async_computation.26 | async-start | bytes 2621440 | tf_op jit(solution)/shard_map/reduce_scatter | solution.py:70
  304.5 56.0 %all-gather.12.cloned.1.call-start = ((), (), s32[]{:S(2)}) async-start(), calls=%async_computation.29 | async-start | bytes 2621440 | tf_op jit(solution)/shard_map/all_gather | solution.py:74
  305.1 80.3 %all-gather.10.cloned.1.call-start = ((), (), s32[]{:S(2)}) async-start(), calls=%async_computation.27 | async-start | bytes 2621440 | tf_op jit(solution)/shard_map/all_gather | solution.py:66
  340.2 92.5 %reduce-scatter.35.cloned.1.call-start = ((), (), s32[]{:S(2)}) async-start(), calls=%async_computation.30 | async-start | bytes 2621440 | tf_op jit(solution)/shard_map/reduce_scatter | solution.py:78
  401.1 66.1 %reduce-scatter.33.cloned.1.call-start = ((), (), s32[]{:S(2)}) async-start(), calls=%async_computation.28 | async-start | bytes 2621440 | tf_op jit(solution)/shard_map/reduce_scatter | solution.py:70
  409.3 60.2 %copy-start.111 = (f32[256,512]{1,0:T(8,128)S(1)}, f32[256,512]{1,0:T(8,128)}, u32[]{:S(2)}) copy-start(f32[256,512]{1,0:T(8,128)} %param.52) | copy-start | bytes 1572868
  409.3 83.9 %all-gather.14.cloned.1.call-start = ((), (), s32[]{:S(2)}) async-start(), calls=%async_computation.31 | async-start | bytes 2621440 | tf_op jit(solution)/shard_map/all_gather | solution.py:74
  470.4 59.8 %reduce-scatter.39.cloned.1.call-start = ((), (), s32[]{:S(2)}) async-start(), calls=%async_computation.33 | async-start | bytes 655360 | tf_op jit(solution)/shard_map/reduce_scatter | solution.py:78
  507.0 34.0 %copy-start.34 = (f32[128,1024]{1,0:T(8,128)S(1)}, f32[128,1024]{1,0:T(8,128)}, u32[]{:S(2)}) copy-start(f32[128,1024]{1,0:T(8,128)} %copy-done.33) | copy-start | bytes 1572868
  508.5 69.7 %reduce-scatter.41.cloned.1.call-start = ((), (), s32[]{:S(2)}) async-start(), calls=%async_computation.34 | async-start | bytes 655360 | tf_op jit(solution)/shard_map/reduce_scatter | solution.py:78
  556.1 66.2 %reduce-scatter.43.cloned.1.call-start = ((), (), s32[]{:S(2)}) async-start(), calls=%async_computation.35 | async-start | bytes 655360 | tf_op jit(solution)/shard_map/reduce_scatter | solution.py:78
  559.3 30.0 %copy-start.107 = (f32[4,128,128]{1,2,0:T(8,128)S(1)}, f32[4,128,128]{1,2,0:T(8,128)}, u32[]{:S(2)}) copy-start(f32[4,128,128]{1,2,0:T(8,128)} %copy-done.106) | copy-start | bytes 786436
  559.3 30.0 %copy-start.207 = (f32[4,128]{1,0:T(4,128)S(1)}, f32[4,128]{1,0:T(4,128)}, u32[]{:S(2)}) copy-start(f32[4,128]{1,0:T(4,128)} %copy-done.206) | copy-start | bytes 6148
  594.2 29.7 %copy-start.265 = (f32[32]{0:T(128)S(1)}, f32[32]{0:T(128)}, u32[]{:S(2)}) copy-start(f32[32]{0:T(128)} %copy-done.264) | copy-start | bytes 388
  596.8 36.0 %copy-start.31 = (f32[128,1024]{1,0:T(8,128)S(1)}, f32[128,1024]{1,0:T(8,128)}, u32[]{:S(2)}) copy-start(f32[128,1024]{1,0:T(8,128)} %copy-done.30) | copy-start | bytes 1572868
  600.1 70.0 %reduce-scatter.45.cloned.1.call-start = ((), (), s32[]{:S(2)}) async-start(), calls=%async_computation.36 | async-start | bytes 655360 | tf_op jit(solution)/shard_map/reduce_scatter | solution.py:78
  640.5 29.7 %copy-start.54 = (f32[32,1024]{1,0:T(8,128)S(1)}, f32[32,1024]{1,0:T(8,128)}, u32[]{:S(2)}) copy-start(f32[32,1024]{1,0:T(8,128)} %copy-done.53) | copy-start | bytes 393220
  640.5 29.7 %copy-start.186 = (f32[1,1024]{1,0:T(1,128)S(1)}, f32[1,1024]{1,0:T(1,128)}, u32[]{:S(2)}) copy-start(f32[1,1024]{1,0:T(1,128)} %copy-done.185) | copy-start | bytes 12292
  640.5 29.7 %copy-start.230 = (f32[32]{0:T(128)S(1)}, f32[32]{0:T(128)}, u32[]{:S(2)}) copy-start(f32[32]{0:T(128)} %copy-done.229) | copy-start | bytes 388
  640.5 29.7 %copy-start.250 = (f32[32]{0:T(128)S(1)}, f32[32]{0:T(128)}, u32[]{:S(2)}) copy-start(f32[32]{0:T(128)} %copy-done.249) | copy-start | bytes 388
  640.5 31.4 %copy-start.263 = (f32[32]{0:T(128)S(1)}, f32[32]{0:T(128)}, u32[]{:S(2)}) copy-start(f32[32]{0:T(128)} %copy-done.262) | copy-start | bytes 388
  640.5 32.5 %copy-start.118 = (f32[32,1024]{1,0:T(8,128)S(1)}, f32[32,1024]{1,0:T(8,128)}, u32[]{:S(2)}) copy-start(f32[32,1024]{1,0:T(8,128)} %copy-done.117) | copy-start | bytes 393220
  647.9 33.4 %copy-start.105 = (f32[4,128,128]{1,2,0:T(8,128)S(1)}, f32[4,128,128]{1,2,0:T(8,128)}, u32[]{:S(2)}) copy-start(f32[4,128,128]{1,2,0:T(8,128)} %copy-done.104) | copy-start | bytes 786436
  647.9 33.4 %copy-start.205 = (f32[4,128]{1,0:T(4,128)S(1)}, f32[4,128]{1,0:T(4,128)}, u32[]{:S(2)}) copy-start(f32[4,128]{1,0:T(4,128)} %copy-done.204) | copy-start | bytes 6148
  648.0 66.3 %reduce-scatter.47.cloned.1.call-start = ((), (), s32[]{:S(2)}) async-start(), calls=%async_computation.37 | async-start | bytes 655360 | tf_op jit(solution)/shard_map/reduce_scatter | solution.py:78
  686.2 29.7 %copy-start.261 = (f32[32]{0:T(128)S(1)}, f32[32]{0:T(128)}, u32[]{:S(2)}) copy-start(f32[32]{0:T(128)} %copy-done.260) | copy-start | bytes 388
  692.1 67.5 %reduce-scatter.49.cloned.1.call-start = ((), (), s32[]{:S(2)}) async-start(), calls=%async_computation.38 | async-start | bytes 655360 | tf_op jit(solution)/shard_map/reduce_scatter | solution.py:78
  737.4 35.2 %copy-start.180 = (f32[1,1024]{1,0:T(1,128)S(1)}, f32[1,1024]{1,0:T(1,128)}, u32[]{:S(2)}) copy-start(f32[1,1024]{1,0:T(1,128)} %copy-done.179) | copy-start | bytes 12292
  737.4 35.2 %copy-start.200 = (f32[4,128]{1,0:T(4,128)S(1)}, f32[4,128]{1,0:T(4,128)}, u32[]{:S(2)}) copy-start(f32[4,128]{1,0:T(4,128)} %copy-done.199) | copy-start | bytes 6148
  737.4 149.6 %reduce-scatter.53.cloned.1.call-start = ((), (), s32[]{:S(2)}) async-start(), calls=%async_computation.40 | async-start | bytes 655360 | tf_op jit(solution)/shard_map/reduce_scatter | solution.py:78
  781.6 108.5 %reduce-scatter.37.cloned.1.call-start = ((), (), s32[]{:S(2)}) async-start(), calls=%async_computation.32 | async-start | bytes 2621440 | tf_op jit(solution)/shard_map/reduce_scatter | solution.py:78
  788.8 101.3 %reduce-scatter.51.cloned.1.call-start = ((), (), s32[]{:S(2)}) async-start(), calls=%async_computation.39 | async-start | bytes 2621440 | tf_op jit(solution)/shard_map/reduce_scatter | solution.py:78
  815.7 1346.1 %all-reduce.5.cloned.1.call-start = ((), (), s32[]{:S(2)}) async-start(), calls=%async_computation.41 | async-start | bytes 80740352 | tf_op jit(solution)/shard_map/psum | solution.py:82
  888.1 58.8 %copy-start.71 = (f32[256,512]{1,0:T(8,128)S(1)}, f32[256,512]{1,0:T(8,128)}, u32[]{:S(2)}) copy-start(f32[256,512]{1,0:T(8,128)} %add_add_fusion.3) | copy-start | bytes 1572868
  890.1 56.9 %copy-start.59 = (f32[256,512]{1,0:T(8,128)S(1)}, f32[256,512]{1,0:T(8,128)}, u32[]{:S(2)}) copy-start(f32[256,512]{1,0:T(8,128)} %reduce-scatter.37.cloned.1.call-done) | copy-start | bytes 1572868
  890.1 56.8 %copy-start.60 = (f32[256,512]{1,0:T(8,128)S(1)}, f32[256,512]{1,0:T(8,128)}, u32[]{:S(2)}) copy-start(f32[256,512]{1,0:T(8,128)} %reduce-scatter.51.cloned.1.call-done) | copy-start | bytes 1572868
  (247 other events, 1711.1 us)
Sparse Core Ops, SparseCore 0:
  13.0 26.4 all-gather.5
  53.9 22.4 reduce-scatter.18
  94.9 22.0 reduce-scatter.20
  133.1 22.0 reduce-scatter.22
  175.3 22.0 reduce-scatter.24
  213.5 22.0 reduce-scatter.26
  237.8 22.5 all-gather.7
  263.6 21.6 reduce-scatter.28
  304.7 31.7 reduce-scatter.30
  338.0 22.5 all-gather.11
  362.8 22.5 all-gather.9
  401.3 31.4 reduce-scatter.34
  435.8 31.3 reduce-scatter.32
  470.5 22.5 all-gather.13
  508.6 21.6 reduce-scatter.38
  556.1 22.0 reduce-scatter.40
  600.2 22.0 reduce-scatter.42
  648.1 22.0 reduce-scatter.44
  692.2 22.0 reduce-scatter.46
  737.5 22.0 reduce-scatter.48
  781.7 22.0 reduce-scatter.52
  806.3 31.4 reduce-scatter.36
  841.1 31.3 reduce-scatter.50
  886.4 1275.2 all-reduce.4
